TPU v7x, 256 devices: a whole 4x4x8 slice. The times are simulated.
256 devices in a mesh: prog: 32 (over z, x), clus: 8 (over y, core).
Axes of the slice: x: 4, y: 4, z: 8, core: 2. Of those that a mesh axis runs over, the one named last changes fastest.
Arguments:
- embeddings: bfloat16 [32768, 2048], P('prog', 'clus'), may hold values from -64 to 64, as said below
- centroids: bfloat16 [4096, 2048], P('clus'), may hold values from -6 to 6, as said below
- plan_grad: bfloat16 [32768, 4096], P('prog', 'clus'), may hold values from -24 to 24
Outputs:
- embed_grad: bfloat16 [32768, 2048], P('prog', 'clus')
- centroid_grad: bfloat16 [4096, 2048], P(('clus', 'prog'))
Inputs may be any that keep to these rules, and one draw needn't show every extreme that they name: embeddings are real-valued with full-rank spread. centroids are real-valued with full-rank spread.
All inputs are finite; a program needn't handle non-finite values.
Results may differ from a plain program's by a relative error of at most 0.006.
Values may be sent and summed in bfloat16 or wider, within the bound.
No kernel may reach another device: no remote copies, remote signals or barrier semaphores. Data moves between devices by JAX's collectives and lax.ppermute only.
A program may use at most 64 MiB of HBM per device.

v0:
```python
import jax
import jax.numpy as jnp
from jax import lax
from jax.sharding import PartitionSpec as P

D = 2048
CENTROIDS = 4096
ITERS = 4


def row_lse(values):
    top = lax.pmax(jnp.max(values, axis=1), "clus")
    total = lax.psum(jnp.sum(jnp.exp(values - top[:, None]), axis=1), "clus")
    return top + jnp.log(total)


def col_lse(values):
    top = lax.pmax(jnp.max(values, axis=0), "prog")
    total = lax.psum(jnp.sum(jnp.exp(values - top[None, :]), axis=0), "prog")
    return top + jnp.log(total)


def shards(embeddings, centroids, plan_grad):
    scale = 1.0 / (0.25 * jnp.sqrt(jnp.float32(D)))
    whole_rows = lax.all_gather(embeddings, "clus", axis=1, tiled=True)
    logits = scale * lax.dot_general(
        whole_rows, centroids, (((1,), (1,)), ((), ())), preferred_element_type=jnp.float32
    )
    total_rows = embeddings.shape[0] * lax.axis_size("prog")
    log_b = jnp.log(jnp.float32(total_rows) / jnp.float32(CENTROIDS))
    col_pot = jnp.zeros((centroids.shape[0],), jnp.float32)
    row_list = []
    col_list = []
    for step in range(ITERS):
        row_pot = -row_lse(logits + col_pot[None, :])
        col_pot = log_b - col_lse(logits + row_pot[:, None])
        row_list.append(row_pot)
        col_list.append(col_pot)
    plan = jnp.exp(logits + row_list[-1][:, None] + col_list[-1][None, :])
    pbar = plan_grad.astype(jnp.float32) * plan
    adjoint = pbar
    col_adj = lax.psum(jnp.sum(pbar, axis=0), "prog")
    direct = jnp.sum(pbar, axis=1)
    for step in range(ITERS - 1, -1, -1):
        weights_a = jnp.exp(logits + row_list[step][:, None] + col_list[step][None, :] - log_b)
        term_a = weights_a * col_adj[None, :]
        adjoint = adjoint - term_a
        row_adj = lax.psum(direct - jnp.sum(term_a, axis=1), "clus")
        direct = jnp.zeros_like(direct)
        if step > 0:
            prev_col = col_list[step - 1]
        else:
            prev_col = jnp.zeros_like(col_pot)
        term_b = jnp.exp(logits + prev_col[None, :] + row_list[step][:, None]) * row_adj[:, None]
        adjoint = adjoint - term_b
        if step > 0:
            col_adj = -lax.psum(jnp.sum(term_b, axis=0), "prog")
    adjoint_b = adjoint.astype(jnp.bfloat16)
    partial_rows = scale * jnp.dot(adjoint_b, centroids, preferred_element_type=jnp.float32)
    embed_grad = lax.psum_scatter(partial_rows, "clus", scatter_dimension=1, tiled=True).astype(
        jnp.bfloat16
    )
    centroid_grad = lax.psum_scatter(
        scale
        * lax.dot_general(
            adjoint_b, whole_rows, (((0,), (0,)), ((), ())), preferred_element_type=jnp.float32
        ),
        "prog",
        scatter_dimension=0,
        tiled=True,
    ).astype(jnp.bfloat16)
    return (embed_grad, centroid_grad)


def solution(mesh):
    placed = (P("prog", "clus"), P("clus", None), P("prog", "clus"))
    return jax.shard_map(
        shards,
        mesh=mesh,
        in_specs=placed,
        out_specs=(P("prog", "clus"), P(("clus", "prog"), None)),
        check_vma=False,
    )
```

profile of v0, /device:TPU:1, one launch (start us, length us, event | category | flops | bytes accessed | tf_op | source)
XLA Modules:
  0.0 1400.4 jit_solution(5728778426446037416)
XLA Ops:
  7.2 0.0 all-gather.2.cloned.1.call-start
  7.2 0.7 all-gather.2.cloned.1.call-update
  7.9 0.0 reduce-scatter.5.cloned.1.call-start
  8.0 1.5 copy.5
  9.5 42.7 %all-gather.2.cloned.1.call-done = bf16[1024,2048]{1,0:T(8,128)(2,1)} async-done(((bf16[1024,256]{1,0:T(8,128)(2,1)}), bf16[1024,2048]{1,0:T(8,128)(2,1)}) %all-gather.2.cloned.1.call-update) | async-done | bytes 4194320 | tf_op jit(solution)/shard_map/all_gather | solution.py:25
  52.1 5.9 fusion.9
  58.0 12.0 pmax.56
  70.0 1.9 exponential_reduce_fusion.7
  71.9 14.3 %psum.112 = f32[1024]{0:T(1024)S(1)} all-reduce(f32[1024]{0:T(1024)S(1)} %exponential_reduce_fusion.7), channel_id=1, replica_groups=mesh['prog'=32,'clus'=8] {'clus'}, use_global_device_ids=true, to_apply=%region_3.0 | all-reduce | flops 1024 | bytes 8192 | tf_op jit(solution)/shard_map/psum | solution.py:13
  86.3 1.8 add_reduce_fusion.6
  88.1 60.9 %pmax.57 = f32[512]{0:T(512)S(1)} all-reduce(f32[512]{0:T(512)S(1)} %add_reduce_fusion.6), channel_id=1, replica_groups=mesh['prog'=32,'clus'=8] {'prog'}, use_global_device_ids=true, to_apply=%region_5.0 | all-reduce | flops 512 | bytes 4096 | tf_op jit(solution)/shard_map/pmax | solution.py:18
  148.9 2.1 exponential_reduce_fusion.6
  151.0 56.1 %psum.113 = f32[512]{0:T(512)S(1)} all-reduce(f32[512]{0:T(512)S(1)} %exponential_reduce_fusion.6), channel_id=1, replica_groups=mesh['prog'=32,'clus'=8] {'prog'}, use_global_device_ids=true, to_apply=%region_7.0 | all-reduce | flops 512 | bytes 4096 | tf_op jit(solution)/shard_map/psum | solution.py:19
  207.1 1.8 add_reduce_fusion.4
  208.9 40.2 %pmax.58 = f32[1024]{0:T(1024)S(1)} all-reduce(f32[1024]{0:T(1024)S(1)} %add_reduce_fusion.4), channel_id=1, replica_groups=mesh['prog'=32,'clus'=8] {'clus'}, use_global_device_ids=true, to_apply=%region_9.0 | all-reduce | flops 1024 | bytes 8192 | tf_op jit(solution)/shard_map/pmax | solution.py:12
  249.1 2.0 exponential_reduce_fusion.5
  251.1 12.4 psum.114
  263.6 1.8 add_reduce_fusion.3
  265.4 57.4 %pmax.59 = f32[512]{0:T(512)S(1)} all-reduce(f32[512]{0:T(512)S(1)} %add_reduce_fusion.3), channel_id=1, replica_groups=mesh['prog'=32,'clus'=8] {'prog'}, use_global_device_ids=true, to_apply=%region_13.0 | all-reduce | flops 512 | bytes 4096 | tf_op jit(solution)/shard_map/pmax | solution.py:18
  322.8 2.1 exponential_reduce_fusion.4
  324.9 56.1 %psum.115 = f32[512]{0:T(512)S(1)} all-reduce(f32[512]{0:T(512)S(1)} %exponential_reduce_fusion.4), channel_id=1, replica_groups=mesh['prog'=32,'clus'=8] {'prog'}, use_global_device_ids=true, to_apply=%region_15.0 | all-reduce | flops 512 | bytes 4096 | tf_op jit(solution)/shard_map/psum | solution.py:19
  381.0 1.8 add_reduce_fusion.2
  382.9 40.1 %pmax.60 = f32[1024]{0:T(1024)S(1)} all-reduce(f32[1024]{0:T(1024)S(1)} %add_reduce_fusion.2), channel_id=1, replica_groups=mesh['prog'=32,'clus'=8] {'clus'}, use_global_device_ids=true, to_apply=%region_17.0 | all-reduce | flops 1024 | bytes 8192 | tf_op jit(solution)/shard_map/pmax | solution.py:12
  423.0 2.0 exponential_reduce_fusion.3
  425.0 12.4 psum.116
  437.4 1.8 add_reduce_fusion.1
  439.2 57.4 %pmax.61 = f32[512]{0:T(512)S(1)} all-reduce(f32[512]{0:T(512)S(1)} %add_reduce_fusion.1), channel_id=1, replica_groups=mesh['prog'=32,'clus'=8] {'prog'}, use_global_device_ids=true, to_apply=%region_21.0 | all-reduce | flops 512 | bytes 4096 | tf_op jit(solution)/shard_map/pmax | solution.py:18
  496.7 2.1 exponential_reduce_fusion.2
  498.8 56.1 %psum.117 = f32[512]{0:T(512)S(1)} all-reduce(f32[512]{0:T(512)S(1)} %exponential_reduce_fusion.2), channel_id=1, replica_groups=mesh['prog'=32,'clus'=8] {'prog'}, use_global_device_ids=true, to_apply=%region_23.0 | all-reduce | flops 512 | bytes 4096 | tf_op jit(solution)/shard_map/psum | solution.py:19
  554.9 1.8 add_reduce_fusion
  556.7 40.1 %pmax.62 = f32[1024]{0:T(1024)S(1)} all-reduce(f32[1024]{0:T(1024)S(1)} %add_reduce_fusion), channel_id=1, replica_groups=mesh['prog'=32,'clus'=8] {'clus'}, use_global_device_ids=true, to_apply=%region_25.0 | all-reduce | flops 1024 | bytes 8192 | tf_op jit(solution)/shard_map/pmax | solution.py:12
  596.8 2.0 exponential_reduce_fusion.1
  598.9 12.4 psum.118
  611.3 1.8 add_reduce_fusion.5
  613.1 57.4 %pmax.63 = f32[512]{0:T(512)S(1)} all-reduce(f32[512]{0:T(512)S(1)} %add_reduce_fusion.5), channel_id=1, replica_groups=mesh['prog'=32,'clus'=8] {'prog'}, use_global_device_ids=true, to_apply=%region_29.0 | all-reduce | flops 512 | bytes 4096 | tf_op jit(solution)/shard_map/pmax | solution.py:18
  670.5 2.1 exponential_reduce_fusion
  672.6 56.2 %psum.119 = f32[512]{0:T(512)S(1)} all-reduce(f32[512]{0:T(512)S(1)} %exponential_reduce_fusion), channel_id=1, replica_groups=mesh['prog'=32,'clus'=8] {'prog'}, use_global_device_ids=true, to_apply=%region_31.0 | all-reduce | flops 512 | bytes 4096 | tf_op jit(solution)/shard_map/psum | solution.py:19
  728.8 2.3 fusion.8
  731.1 57.0 %psum.120 = f32[512]{0:T(512)S(1)} all-reduce(f32[512]{0:T(512)S(1)} %get-tuple-element.2), channel_id=1, replica_groups=mesh['prog'=32,'clus'=8] {'prog'}, use_global_device_ids=true, to_apply=%region_33.0 | all-reduce | flops 512 | bytes 4096 | tf_op jit(solution)/shard_map/psum | solution.py:42
  788.1 2.1 fusion.4
  790.3 54.7 %psum.121 = f32[1024]{0:T(1024)S(1)} all-reduce(f32[1024]{0:T(1024)S(1)} %sub.146), channel_id=1, replica_groups=mesh['prog'=32,'clus'=8] {'clus'}, use_global_device_ids=true, to_apply=%region_36.0 | all-reduce | flops 1024 | bytes 8192 | tf_op jit(solution)/shard_map/psum | solution.py:48
  845.0 2.2 fusion.1
  847.1 55.9 %psum.122 = f32[512]{0:T(512)S(1)} all-reduce(f32[512]{0:T(512)S(1)} %fusion.1), channel_id=1, replica_groups=mesh['prog'=32,'clus'=8] {'prog'}, use_global_device_ids=true, to_apply=%region_38.0 | all-reduce | flops 512 | bytes 4096 | tf_op jit(solution)/shard_map/psum | solution.py:57
  903.0 2.1 fusion.5
  905.2 26.4 %psum.123 = f32[1024]{0:T(1024)S(1)} all-reduce(f32[1024]{0:T(1024)S(1)} %broadcast_subtract_fusion.2), channel_id=1, replica_groups=mesh['prog'=32,'clus'=8] {'clus'}, use_global_device_ids=true, to_apply=%region_40.0 | all-reduce | flops 1024 | bytes 8192 | tf_op jit(solution)/shard_map/psum | solution.py:48
  931.6 2.2 fusion.2
  933.7 57.4 %psum.124 = f32[512]{0:T(512)S(1)} all-reduce(f32[512]{0:T(512)S(1)} %fusion.2), channel_id=1, replica_groups=mesh['prog'=32,'clus'=8] {'prog'}, use_global_device_ids=true, to_apply=%region_42.0 | all-reduce | flops 512 | bytes 4096 | tf_op jit(solution)/shard_map/psum | solution.py:57
  991.2 2.1 fusion.6
  993.3 26.6 %psum.125 = f32[1024]{0:T(1024)S(1)} all-reduce(f32[1024]{0:T(1024)S(1)} %broadcast_subtract_fusion.1), channel_id=1, replica_groups=mesh['prog'=32,'clus'=8] {'clus'}, use_global_device_ids=true, to_apply=%region_44.0 | all-reduce | flops 1024 | bytes 8192 | tf_op jit(solution)/shard_map/psum | solution.py:48
  1019.9 2.2 fusion.3
  1022.1 55.7 %psum.126 = f32[512]{0:T(512)S(1)} all-reduce(f32[512]{0:T(512)S(1)} %fusion.3), channel_id=1, replica_groups=mesh['prog'=32,'clus'=8] {'prog'}, use_global_device_ids=true, to_apply=%region_46.0 | all-reduce | flops 512 | bytes 4096 | tf_op jit(solution)/shard_map/psum | solution.py:57
  1077.8 2.1 fusion
  1080.0 26.4 %psum.127 = f32[1024]{0:T(1024)S(1)} all-reduce(f32[1024]{0:T(1024)S(1)} %broadcast_subtract_fusion), channel_id=1, replica_groups=mesh['prog'=32,'clus'=8] {'clus'}, use_global_device_ids=true, to_apply=%region_48.0 | all-reduce | flops 1024 | bytes 8192 | tf_op jit(solution)/shard_map/psum | solution.py:48
  1106.4 6.2 subtract_convert_fusion
  1112.6 1.0 copy-done.2
  1113.6 4.3 convolution_multiply_fusion.1
  1118.0 0.0 reduce-scatter.3.cloned.1.call-start
  1118.0 1.1 copy-done.3
  1119.2 5.6 convolution_multiply_fusion
  1124.8 0.0 reduce-scatter.3.cloned.1.call-update
  1124.8 206.5 %reduce-scatter.5.cloned.1.call-done = f32[16,2048]{1,0:T(8,128)} async-done(((f32[512,2048]{1,0:T(8,128)}), f32[16,2048]{1,0:T(8,128)}) %reduce-scatter.5.cloned.1.call-update) | async-done | bytes 131088 | tf_op jit(solution)/shard_map/reduce_scatter | solution.py:63
  1331.3 1.5 convert_element_type.15
  1332.8 59.0 %reduce-scatter.3.cloned.1.call-done = f32[1024,256]{1,0:T(8,128)} async-done(((f32[1024,2048]{1,0:T(8,128)}), f32[1024,256]{1,0:T(8,128)}) %reduce-scatter.3.cloned.1.call-update) | async-done | bytes 1048592 | tf_op jit(solution)/shard_map/reduce_scatter | solution.py:60
  1391.8 2.1 convert_element_type.14
  (22 shorter events, 0.1 us)
Async XLA Ops:
  7.2 45.0 %copy-start = (bf16[512,2048]{1,0:T(8,128)(2,1)S(1)}, bf16[512,2048]{1,0:T(8,128)(2,1)}, u32[]{:S(2)}) copy-start(bf16[512,2048]{1,0:T(8,128)(2,1)} %param.4) | copy-start | bytes 6291460
  7.2 45.0 %all-gather.2.cloned.1.call-start = ((), (), s32[]{:S(2)}) async-start(), calls=%async_computation.2 | async-start | bytes 4718592 | tf_op jit(solution)/shard_map/all_gather | solution.py:25
  7.9 1323.4 %reduce-scatter.5.cloned.1.call-start = ((), (), s32[]{:S(2)}) async-start(), calls=%async_computation.4 | async-start | bytes 4325376 | tf_op jit(solution)/shard_map/reduce_scatter | solution.py:63
  1106.4 7.2 copy-start.1
  1112.6 1.0 copy-start.2
  1117.9 1.2 copy-start.3
  1118.0 273.8 %reduce-scatter.3.cloned.1.call-start = ((), (), s32[]{:S(2)}) async-start(), calls=%async_computation.3 | async-start | bytes 9437184 | tf_op jit(solution)/shard_map/reduce_scatter | solution.py:60
Sparse Core Ops, SparseCore 0:
  9.8 42.2 all-gather.1
  1118.1 213.1 reduce-scatter.4
  1333.8 57.9 reduce-scatter.2
where the time goes:
time: 1400 us
  blocking collectives  1000 us (71%)
  waiting for transfers between devices  309 us (22%)
  other arithmetic  56.3 us (4%)
  matrix products  15.8 us (1%)
    pmax x4, blocking collectives, col_lse(): top = lax.pmax(jnp.max(values, axis=0), 'prog')  233 us
    psum x4, blocking collectives, col_lse(): total = lax.psum(jnp.sum(jnp.exp(values - top[None, :]), axis=0), 'prog')  225 us
    reduce_scatter x1, waiting for transfers between devices, shards(): lax.psum_scatter(scale * lax.dot_general(adjoint_b, whole_rows, (((0,), (...  206 us
    psum x3, blocking collectives, shards(): col_adj = -lax.psum(jnp.sum(term_b, axis=0), 'prog')  169 us
    psum x4, blocking collectives, shards(): row_adj = lax.psum(direct - jnp.sum(term_a, axis=1), 'clus')  134 us
    pmax x4, blocking collectives, row_lse(): top = lax.pmax(jnp.max(values, axis=1), 'clus')  132 us
    reduce_scatter x1, waiting for transfers between devices, shards(): lax.psum_scatter(partial_rows, 'clus', scatter_dimension=1, tiled=True)  59 us
    psum x1, blocking collectives, shards(): col_adj = lax.psum(jnp.sum(pbar, axis=0), 'prog')  57 us
  transfers between devices with their start and end apart: 3, of which 3 were waited for; matrix products, arithmetic and copies ran while one was open for 1% of the time, Pallas kernels for 0%

commit v1 on v0

--- a/solution.py
+++ b/solution.py
@@ -8,6 +8,12 @@
 ITERS = 4
 
 
+def add_all(block, mesh_axis):
+    parts = lax.all_gather(block, mesh_axis, axis=0, tiled=False)
+    acc = parts.sum(axis=0)
+    return acc
+
+
 def row_lse(values):
     top = lax.pmax(jnp.max(values, axis=1), "clus")
     total = lax.psum(jnp.sum(jnp.exp(values - top[:, None]), axis=1), "clus")
@@ -16,7 +22,7 @@
 
 def col_lse(values):
     top = lax.pmax(jnp.max(values, axis=0), "prog")
-    total = lax.psum(jnp.sum(jnp.exp(values - top[None, :]), axis=0), "prog")
+    total = add_all(jnp.sum(jnp.exp(values - top[None, :]), axis=0), "prog")
     return top + jnp.log(total)
 
 

time: 1400 us -> 1310 us (0.936)
  blocking collectives: 1000 us -> 909 us
    psum x4 -> x0, blocking collectives: 225 us -> none  [col_lse(): total = lax.psum(jnp.sum(jnp.exp(values - top[None, :]), axis=0), 'prog')]
    all_gather x0 -> x4, blocking collectives: none -> 134 us  [add_all(): parts = lax.all_gather(block, mesh_axis, axis=0, tiled=False)]
where the time goes in v1:
time: 1310 us
  blocking collectives  909 us (69%)
  waiting for transfers between devices  309 us (24%)
  other arithmetic  56.6 us (4%)
  matrix products  15.8 us (1%)
  between operations  13.9 us (1%)
    pmax x4, blocking collectives, col_lse(): top = lax.pmax(jnp.max(values, axis=0), 'prog')  235 us
    reduce_scatter x1, waiting for transfers between devices, shards(): lax.psum_scatter(scale * lax.dot_general(adjoint_b, whole_rows, (((0,), (...  207 us
    psum x3, blocking collectives, shards(): col_adj = -lax.psum(jnp.sum(term_b, axis=0), 'prog')  169 us
    all_gather x4, blocking collectives, add_all(): parts = lax.all_gather(block, mesh_axis, axis=0, tiled=False)  134 us
    psum x4, blocking collectives, shards(): row_adj = lax.psum(direct - jnp.sum(term_a, axis=1), 'clus')  132 us
    pmax x4, blocking collectives, row_lse(): top = lax.pmax(jnp.max(values, axis=1), 'clus')  128 us
    reduce_scatter x1, waiting for transfers between devices, shards(): lax.psum_scatter(partial_rows, 'clus', scatter_dimension=1, tiled=True)  58.5 us
    psum x1, blocking collectives, shards(): col_adj = lax.psum(jnp.sum(pbar, axis=0), 'prog')  58.1 us
  transfers between devices with their start and end apart: 3, of which 3 were waited for; matrix products, arithmetic and copies ran while one was open for 1% of the time, Pallas kernels for 0%

profile of v1, /device:TPU:1, one launch (start us, length us, event | category | flops | bytes accessed | tf_op | source)
XLA Modules:
  0.0 1307.6 jit_solution(8836760041979009753)
XLA Ops:
  7.2 0.7 all-gather.10.cloned.1.call-update
  8.0 1.5 copy.6
  9.5 42.7 %all-gather.10.cloned.1.call-done = bf16[1024,2048]{1,0:T(8,128)(2,1)} async-done(((bf16[1024,256]{1,0:T(8,128)(2,1)}), bf16[1024,2048]{1,0:T(8,128)(2,1)}) %all-gather.10.cloned.1.call-update) | async-done | bytes 4194320 | tf_op jit(solution)/shard_map/all_gather | solution.py:31
  52.1 5.9 fusion.9
  58.0 12.0 pmax.56
  70.0 1.9 exponential_reduce_fusion.7
  71.9 14.3 %psum.84 = f32[1024]{0:T(1024)S(1)} all-reduce(f32[1024]{0:T(1024)S(1)} %exponential_reduce_fusion.7), channel_id=1, replica_groups=mesh['prog'=32,'clus'=8] {'clus'}, use_global_device_ids=true, to_apply=%region_3.0 | all-reduce | flops 1024 | bytes 8192 | tf_op jit(solution)/shard_map/psum | solution.py:19
  86.3 1.8 add_reduce_fusion.6
  88.1 60.9 %pmax.57 = f32[512]{0:T(512)S(1)} all-reduce(f32[512]{0:T(512)S(1)} %add_reduce_fusion.6), channel_id=1, replica_groups=mesh['prog'=32,'clus'=8] {'prog'}, use_global_device_ids=true, to_apply=%region_5.0 | all-reduce | flops 512 | bytes 4096 | tf_op jit(solution)/shard_map/pmax | solution.py:24
  148.9 2.1 exponential_reduce_fusion.6
  151.0 33.9 %all-gather.4 = f32[32,1,512]{2,1,0:T(1,128)S(1)} all-gather(f32[1,1,512]{2,1,0:T(1,128)S(1)} %bitcast.10), channel_id=2, replica_groups=mesh['prog'=32,'clus'=8] {'prog'}, dimensions={0}, use_global_device_ids=true | all-gather | bytes 67584 | tf_op jit(solution)/shard_map/all_gather | solution.py:12
  184.9 0.1 reduce_sum.191
  185.0 1.8 add_reduce_fusion.4
  186.8 38.4 %pmax.58 = f32[1024]{0:T(1024)S(1)} all-reduce(f32[1024]{0:T(1024)S(1)} %add_reduce_fusion.4), channel_id=1, replica_groups=mesh['prog'=32,'clus'=8] {'clus'}, use_global_device_ids=true, to_apply=%region_9.0 | all-reduce | flops 1024 | bytes 8192 | tf_op jit(solution)/shard_map/pmax | solution.py:18
  225.2 2.0 exponential_reduce_fusion.5
  227.3 12.4 psum.85
  239.7 1.8 add_reduce_fusion.3
  241.5 58.1 %pmax.59 = f32[512]{0:T(512)S(1)} all-reduce(f32[512]{0:T(512)S(1)} %add_reduce_fusion.3), channel_id=1, replica_groups=mesh['prog'=32,'clus'=8] {'prog'}, use_global_device_ids=true, to_apply=%region_13.0 | all-reduce | flops 512 | bytes 4096 | tf_op jit(solution)/shard_map/pmax | solution.py:24
  299.6 2.1 exponential_reduce_fusion.4
  301.7 33.5 %all-gather.5 = f32[32,1,512]{2,1,0:T(1,128)S(1)} all-gather(f32[1,1,512]{2,1,0:T(1,128)S(1)} %bitcast.11), channel_id=3, replica_groups=mesh['prog'=32,'clus'=8] {'prog'}, dimensions={0}, use_global_device_ids=true | all-gather | bytes 67584 | tf_op jit(solution)/shard_map/all_gather | solution.py:12
  335.2 0.1 reduce_sum.194
  335.3 1.8 add_reduce_fusion.2
  337.1 38.8 %pmax.60 = f32[1024]{0:T(1024)S(1)} all-reduce(f32[1024]{0:T(1024)S(1)} %add_reduce_fusion.2), channel_id=1, replica_groups=mesh['prog'=32,'clus'=8] {'clus'}, use_global_device_ids=true, to_apply=%region_17.0 | all-reduce | flops 1024 | bytes 8192 | tf_op jit(solution)/shard_map/pmax | solution.py:18
  375.9 2.0 exponential_reduce_fusion.3
  377.9 12.4 psum.86
  390.4 1.8 add_reduce_fusion.1
  392.2 58.1 %pmax.61 = f32[512]{0:T(512)S(1)} all-reduce(f32[512]{0:T(512)S(1)} %add_reduce_fusion.1), channel_id=1, replica_groups=mesh['prog'=32,'clus'=8] {'prog'}, use_global_device_ids=true, to_apply=%region_21.0 | all-reduce | flops 512 | bytes 4096 | tf_op jit(solution)/shard_map/pmax | solution.py:24
  450.3 2.1 exponential_reduce_fusion.2
  452.4 33.5 %all-gather.6 = f32[32,1,512]{2,1,0:T(1,128)S(1)} all-gather(f32[1,1,512]{2,1,0:T(1,128)S(1)} %bitcast.12), channel_id=4, replica_groups=mesh['prog'=32,'clus'=8] {'prog'}, dimensions={0}, use_global_device_ids=true | all-gather | bytes 67584 | tf_op jit(solution)/shard_map/all_gather | solution.py:12
  485.9 0.1 reduce_sum.197
  486.0 1.8 add_reduce_fusion
  487.8 38.8 %pmax.62 = f32[1024]{0:T(1024)S(1)} all-reduce(f32[1024]{0:T(1024)S(1)} %add_reduce_fusion), channel_id=1, replica_groups=mesh['prog'=32,'clus'=8] {'clus'}, use_global_device_ids=true, to_apply=%region_25.0 | all-reduce | flops 1024 | bytes 8192 | tf_op jit(solution)/shard_map/pmax | solution.py:18
  526.6 2.0 exponential_reduce_fusion.1
  528.6 12.4 psum.87
  541.0 1.8 add_reduce_fusion.5
  542.8 58.1 %pmax.63 = f32[512]{0:T(512)S(1)} all-reduce(f32[512]{0:T(512)S(1)} %add_reduce_fusion.5), channel_id=1, replica_groups=mesh['prog'=32,'clus'=8] {'prog'}, use_global_device_ids=true, to_apply=%region_29.0 | all-reduce | flops 512 | bytes 4096 | tf_op jit(solution)/shard_map/pmax | solution.py:24
  600.9 2.1 exponential_reduce_fusion
  603.0 33.5 %all-gather.7 = f32[32,1,512]{2,1,0:T(1,128)S(1)} all-gather(f32[1,1,512]{2,1,0:T(1,128)S(1)} %bitcast.13), channel_id=5, replica_groups=mesh['prog'=32,'clus'=8] {'prog'}, dimensions={0}, use_global_device_ids=true | all-gather | bytes 67584 | tf_op jit(solution)/shard_map/all_gather | solution.py:12
  636.5 0.1 reduce_sum.200
  636.6 2.3 fusion.8
  638.9 58.1 %psum.88 = f32[512]{0:T(512)S(1)} all-reduce(f32[512]{0:T(512)S(1)} %get-tuple-element.2), channel_id=1, replica_groups=mesh['prog'=32,'clus'=8] {'prog'}, use_global_device_ids=true, to_apply=%region_33.0 | all-reduce | flops 512 | bytes 4096 | tf_op jit(solution)/shard_map/psum | solution.py:48
  697.0 2.1 fusion.4
  699.2 53.1 %psum.89 = f32[1024]{0:T(1024)S(1)} all-reduce(f32[1024]{0:T(1024)S(1)} %sub.146), channel_id=1, replica_groups=mesh['prog'=32,'clus'=8] {'clus'}, use_global_device_ids=true, to_apply=%region_36.0 | all-reduce | flops 1024 | bytes 8192 | tf_op jit(solution)/shard_map/psum | solution.py:54
  752.3 2.2 fusion.1
  754.5 55.7 %psum.90 = f32[512]{0:T(512)S(1)} all-reduce(f32[512]{0:T(512)S(1)} %fusion.1), channel_id=1, replica_groups=mesh['prog'=32,'clus'=8] {'prog'}, use_global_device_ids=true, to_apply=%region_38.0 | all-reduce | flops 512 | bytes 4096 | tf_op jit(solution)/shard_map/psum | solution.py:63
  810.2 2.1 fusion.5
  812.4 26.3 %psum.91 = f32[1024]{0:T(1024)S(1)} all-reduce(f32[1024]{0:T(1024)S(1)} %broadcast_subtract_fusion.2), channel_id=1, replica_groups=mesh['prog'=32,'clus'=8] {'clus'}, use_global_device_ids=true, to_apply=%region_40.0 | all-reduce | flops 1024 | bytes 8192 | tf_op jit(solution)/shard_map/psum | solution.py:54
  838.7 2.2 fusion.2
  840.9 57.4 %psum.92 = f32[512]{0:T(512)S(1)} all-reduce(f32[512]{0:T(512)S(1)} %fusion.2), channel_id=1, replica_groups=mesh['prog'=32,'clus'=8] {'prog'}, use_global_device_ids=true, to_apply=%region_42.0 | all-reduce | flops 512 | bytes 4096 | tf_op jit(solution)/shard_map/psum | solution.py:63
  898.3 2.1 fusion.6
  900.5 26.6 %psum.93 = f32[1024]{0:T(1024)S(1)} all-reduce(f32[1024]{0:T(1024)S(1)} %broadcast_subtract_fusion.1), channel_id=1, replica_groups=mesh['prog'=32,'clus'=8] {'clus'}, use_global_device_ids=true, to_apply=%region_44.0 | all-reduce | flops 1024 | bytes 8192 | tf_op jit(solution)/shard_map/psum | solution.py:54
  927.1 2.2 fusion.3
  929.3 55.7 %psum.94 = f32[512]{0:T(512)S(1)} all-reduce(f32[512]{0:T(512)S(1)} %fusion.3), channel_id=1, replica_groups=mesh['prog'=32,'clus'=8] {'prog'}, use_global_device_ids=true, to_apply=%region_46.0 | all-reduce | flops 512 | bytes 4096 | tf_op jit(solution)/shard_map/psum | solution.py:63
  985.0 2.1 fusion
  987.2 26.3 %psum.95 = f32[1024]{0:T(1024)S(1)} all-reduce(f32[1024]{0:T(1024)S(1)} %broadcast_subtract_fusion), channel_id=1, replica_groups=mesh['prog'=32,'clus'=8] {'clus'}, use_global_device_ids=true, to_apply=%region_48.0 | all-reduce | flops 1024 | bytes 8192 | tf_op jit(solution)/shard_map/psum | solution.py:54
  1013.5 6.3 subtract_convert_fusion
  1019.8 1.0 copy-done.2
  1020.8 4.3 convolution_multiply_fusion.1
  1025.2 1.1 copy-done.3
  1026.3 5.6 convolution_multiply_fusion
  1032.0 206.9 %reduce-scatter.5.cloned.1.call-done = f32[16,2048]{1,0:T(8,128)} async-done(((f32[512,2048]{1,0:T(8,128)}), f32[16,2048]{1,0:T(8,128)}) %reduce-scatter.5.cloned.1.call-update) | async-done | bytes 131088 | tf_op jit(solution)/shard_map/reduce_scatter | solution.py:69
  1238.9 1.5 convert_element_type.15
  1240.4 58.5 %reduce-scatter.3.cloned.1.call-done = f32[1024,256]{1,0:T(8,128)} async-done(((f32[1024,2048]{1,0:T(8,128)}), f32[1024,256]{1,0:T(8,128)}) %reduce-scatter.3.cloned.1.call-update) | async-done | bytes 1048592 | tf_op jit(solution)/shard_map/reduce_scatter | solution.py:66
  1299.0 2.1 convert_element_type.14
  (26 shorter events, 0.3 us)
Async XLA Ops:
  7.2 45.0 %copy-start = (bf16[512,2048]{1,0:T(8,128)(2,1)S(1)}, bf16[512,2048]{1,0:T(8,128)(2,1)}, u32[]{:S(2)}) copy-start(bf16[512,2048]{1,0:T(8,128)(2,1)} %param.4) | copy-start | bytes 6291460
  7.2 45.0 %all-gather.10.cloned.1.call-start = ((), (), s32[]{:S(2)}) async-start(), calls=%async_computation.2 | async-start | bytes 4718592 | tf_op jit(solution)/shard_map/all_gather | solution.py:31
  7.9 1231.0 %reduce-scatter.5.cloned.1.call-start = ((), (), s32[]{:S(2)}) async-start(), calls=%async_computation.4 | async-start | bytes 4325376 | tf_op jit(solution)/shard_map/reduce_scatter | solution.py:69
  1013.5 7.2 copy-start.1
  1019.8 1.0 copy-start.2
  1025.1 1.2 copy-start.3
  1025.1 273.8 %reduce-scatter.3.cloned.1.call-start = ((), (), s32[]{:S(2)}) async-start(), calls=%async_computation.3 | async-start | bytes 9437184 | tf_op jit(solution)/shard_map/reduce_scatter | solution.py:66
Sparse Core Ops, SparseCore 0:
  9.8 42.2 all-gather.9
  1025.2 213.5 reduce-scatter.4
  1241.4 57.4 reduce-scatter.2
